TPU v7x, 256 devices: a whole 4x4x8 slice. The times are simulated.
256 devices in a mesh: rows: 8 (over x, core), cols: 32 (over y, z).
Axes of the slice: x: 4, y: 4, z: 8, core: 2. Of those that a mesh axis runs over, the one named last changes fastest.
Arguments:
- features: bfloat16 [256, 4096, 1536], P('rows', 'cols'), may hold values from -6 to 6
- projection: bfloat16 [1536, 128], replicated, may hold values from -0.4375 to 0.4375
- prev_dist: float32 [256, 4096], P('rows', 'cols'), may hold values from 0.5 to 3
- valid: int32 [256, 4096], P('rows', 'cols'), may hold values 0 or 1
- pick_owner: int32 [512], replicated, may hold values from 0 to 255, as said below
- pick_slot: int32 [512], replicated, may hold values from 0 to 4095, as said below
Outputs:
- min_dist: float32 [256, 4096], P('rows', 'cols')
Inputs may be any that keep to these rules, and one draw needn't show every extreme that they name: `pick_owner`: no two picks name the same patch; picks fall on devices at random. `pick_slot`: see pick_owner.
All inputs are finite; a program needn't handle non-finite values. No bound on the sum of `valid` on one device may be relied on, other than what follows from the above.
Results may differ from a plain program's by a relative error of at most 0.0003.
Values may be sent and summed in bfloat16 or wider, within the bound.
A program may use at most 128 MiB of HBM per device.

v0:
```python
import jax
import jax.numpy as jnp
from jax import lax
from jax.sharding import PartitionSpec as P

D_PROJ = 128


def padded_2(block, sides, width):
    for axis, dim in sides:
        count = lax.axis_size(axis)
        forward = [(i, i + 1) for i in range(count - 1)]
        backward = [(target, source) for source, target in forward]
        low = lax.ppermute(
            lax.slice_in_dim(block, block.shape[dim] - width, None, axis=dim), axis, forward
        )
        high = lax.ppermute(lax.slice_in_dim(block, 0, width, axis=dim), axis, backward)
        block = jnp.concatenate([low, block, high], axis=dim)
    return block


def window_sum(padded, rows_dev, cols_dev):
    total = jnp.zeros((rows_dev, cols_dev, padded.shape[2]), jnp.float32)
    for row_off in range(3):
        for col_off in range(3):
            total = total + padded[
                row_off : row_off + rows_dev, col_off : col_off + cols_dev
            ].astype(jnp.float32)
    return total / 9.0


def shards(features, projection, prev_dist, valid, pick_owner, pick_slot):
    rows_dev, cols_dev, channels = features.shape
    proj_full = projection.astype(jnp.float32)
    own_index = lax.axis_index("rows") * lax.axis_size("cols") + lax.axis_index("cols")
    owned = pick_owner == own_index
    padded = padded_2(features, (("rows", 0), ("cols", 1)), 1)
    pooled = window_sum(padded, rows_dev, cols_dev).reshape(rows_dev * cols_dev, channels)
    projected = jnp.dot(pooled, proj_full, precision=lax.Precision.HIGHEST)
    local_rows = jnp.where(owned[:, None], projected[pick_slot], jnp.float32(0.0))
    pick_rows = lax.psum(local_rows, ("rows", "cols"))
    pick_sq = jnp.sum(pick_rows * pick_rows, axis=1)
    own_sq = jnp.sum(projected * projected, axis=1)
    inner_prod = jnp.dot(projected, pick_rows.T, precision=lax.Precision.HIGHEST)
    scaled_gap = (own_sq[:, None] + pick_sq[None, :] - 2.0 * inner_prod) / D_PROJ
    nearest = jnp.min(scaled_gap, axis=1).reshape(rows_dev, cols_dev)
    return jnp.where(valid == 1, jnp.minimum(prev_dist, nearest), jnp.float32(0.0))


def solution(mesh):
    return jax.shard_map(
        shards,
        mesh=mesh,
        in_specs=(P("rows", "cols", None), P(), P("rows", "cols"), P("rows", "cols"), P(), P()),
        out_specs=P("rows", "cols"),
        check_vma=False,
    )
```

profile of v0, /device:TPU:1, one launch (start us, length us, event | category | flops | bytes accessed | tf_op | source)
XLA Modules:
  0.0 381.6 jit_solution(17740806826330092399)
XLA Ops:
  6.5 0.0 copy-start
  6.5 0.0 all-reduce.2.cloned.1.call-start
  6.5 1.2 fusion.6
  7.8 4.5 %collective-permute-start = (bf16[1,128,1536]{2,1,0:T(8,128)(2,1)S(1)}, bf16[1,128,1536]{2,1,0:T(8,128)(2,1)S(1)}, u32[]{:S(2)}, u32[]{:S(2)}) collective-permute-start(bf16[1,128,1536]{2,1,0:T(8,128)(2,1)S(1)} %get-tuple-element.8), channel_id=1, source_target_pairs={{0,32},{32,64},{64,96},{96,128},{128,160},{160,192},{192,224},{1,3... | collective-permute-start | bytes 1179656 | tf_op jit(solution)/shard_map/ppermute | solution.py:14
  12.3 2.0 collective-permute-start.1
  14.2 0.7 broadcast_compare_fusion
  14.9 0.7 compare_select_fusion
  15.6 1.4 collective-permute-done
  17.0 6.7 %constant_dynamic-update-slice_fusion.1 = bf16[34,128,1536]{2,1,0:T(8,128)(2,1)S(1)} fusion(bf16[34,128,1536]{2,1,0:T(8,128)(2,1)S(1)} %constant_dynamic-update-slice_fusion.2, bf16[32,128,1536]{2,1,0:T(8,128)(2,1)} %param.6), kind=kLoop, calls=%fused_computation.25 | loop fusion | bytes 25165824
  23.7 0.0 collective-permute-done.1
  23.7 0.0 copy-start.1
  23.7 4.8 %copy-done.1 = bf16[34,128,1536]{2,1,0:T(8,128)(2,1)} copy-done((bf16[34,128,1536]{2,1,0:T(8,128)(2,1)}, bf16[34,128,1536]{2,1,0:T(8,128)(2,1)S(1)}, u32[]{:S(2)}) %copy-start.1) | copy-done | bytes 13369368
  28.6 0.3 fusion.5
  28.9 3.5 collective-permute-start.2
  32.5 1.3 collective-permute-start.3
  33.8 0.5 collective-permute-done.2
  34.3 0.2 copy.16
  34.5 3.8 %collective-permute-done.3 = bf16[34,1,1536]{2,0,1:T(8,128)(2,1)S(1)} collective-permute-done((bf16[34,1,1536]{2,0,1:T(8,128)(2,1)S(1)}, bf16[34,1,1536]{2,0,1:T(8,128)(2,1)S(1)}, u32[]{:S(2)}, u32[]{:S(2)}) %collective-permute-start.3) | collective-permute-done | bytes 104480 | tf_op jit(solution)/shard_map/ppermute | solution.py:17
  38.3 0.2 copy.18
  38.5 47.2 %add_multiply_fusion = f32[32,128,1536]{2,1,0:T(8,128)} fusion(bf16[32,128,1536]{2,1,0:T(8,128)(2,1)} %param.6, bf16[34,128,1536]{2,1,0:T(8,128)(2,1)} %copy-done.1, bf16[34,1,1536]{2,1,0:T(2,128)(2,1)S(1)} %copy.18, bf16[34,1,1536]{2,1,0:T(2,128)(2,1)S(1)} %copy.16, bf16[1,128,1536]{2,1,0:T(8,128)(2,1)S(1)} %collective-permute-done.1, ...), kind=kLoop, calls=%fused_computation.1 | loop fusion | flops 264241152 | bytes 52113408 | tf_op jit(solution)/shard_map/div | solution.py:29
  85.7 0.0 copy-done
  85.7 18.7 %multiply_reduce_fusion.1 = (f32[4096]{0:T(1024)S(1)}, f32[4096,128]{0,1:T(8,128)S(1)}) fusion(f32[4096,1536]{1,0:T(8,128)} %bitcast.9, bf16[1536,128]{1,0:T(8,128)(2,1)S(1)} %copy-done), kind=kOutput, calls=%fused_computation.19 | convolution fusion | flops 9664720896 | bytes 27672576 | tf_op jit(solution)/shard_map/dot_general | solution.py:39
  104.5 0.0 copy-start.2
  104.5 0.0 copy-start.3
  104.5 1.9 copy.19
  106.4 2.6 gather_fusion
  109.0 0.8 broadcast_select_fusion
  109.8 0.0 all-reduce.2.cloned.1.call-update
  109.9 253.9 %all-reduce.2.cloned.1.call-done = f32[512,128]{1,0:T(8,128)} async-done(((f32[512,128]{1,0:T(8,128)}), f32[512,128]{1,0:T(8,128)}) %all-reduce.2.cloned.1.call-update) | async-done | bytes 262160 | tf_op jit(solution)/shard_map/psum | solution.py:41
  363.8 1.1 multiply_reduce_fusion.2
  364.9 9.2 %multiply_reduce_fusion = f32[4096]{0:T(1024)S(1)} fusion(f32[4096,128]{0,1:T(8,128)S(1)} %get-tuple-element.10, f32[512,128]{1,0:T(8,128)} %all-reduce.2.cloned.1.call-done, f32[512]{0:T(512)S(1)} %multiply_reduce_fusion.2, f32[4096]{0:T(1024)S(1)} %get-tuple-element.9), kind=kOutput, calls=%fused_computation.18 | convolution fusion | flops 3231707136 | bytes 2394112 | tf_op jit(solution)/shard_map/dot_general | solution.py:44
  374.1 0.6 fusion.4
  (7 shorter events, 0.1 us)
Async XLA Ops:
  6.5 79.2 %copy-start = (bf16[1536,128]{1,0:T(8,128)(2,1)S(1)}, bf16[1536,128]{1,0:T(8,128)(2,1)}, u32[]{:S(2)}) copy-start(bf16[1536,128]{1,0:T(8,128)(2,1)} %param.7) | copy-start | bytes 1179652
  6.5 357.2 %all-reduce.2.cloned.1.call-start = ((), (), s32[]{:S(2)}) async-start(), calls=%async_computation | async-start | bytes 524288 | tf_op jit(solution)/shard_map/psum | solution.py:41
  7.8 9.2 %collective-permute-start = (bf16[1,128,1536]{2,1,0:T(8,128)(2,1)S(1)}, bf16[1,128,1536]{2,1,0:T(8,128)(2,1)S(1)}, u32[]{:S(2)}, u32[]{:S(2)}) collective-permute-start(bf16[1,128,1536]{2,1,0:T(8,128)(2,1)S(1)} %get-tuple-element.8), channel_id=1, source_target_pairs={{0,32},{32,64},{64,96},{96,128},{128,160},{160,192},{192,224},{1,3... | collective-permute-start | bytes 1179656 | tf_op jit(solution)/shard_map/ppermute | solution.py:14
  12.3 11.4 %collective-permute-start.1 = (bf16[1,128,1536]{2,1,0:T(8,128)(2,1)S(1)}, bf16[1,128,1536]{2,1,0:T(8,128)(2,1)S(1)}, u32[]{:S(2)}, u32[]{:S(2)}) collective-permute-start(bf16[1,128,1536]{2,1,0:T(8,128)(2,1)S(1)} %get-tuple-element.7), channel_id=1, source_target_pairs={{32,0},{64,32},{96,64},{128,96},{160,128},{192,160},{224,192},{33,... | collective-permute-start | bytes 1179656 | tf_op jit(solution)/shard_map/ppermute | solution.py:17
  23.7 4.8 %copy-start.1 = (bf16[34,128,1536]{2,1,0:T(8,128)(2,1)}, bf16[34,128,1536]{2,1,0:T(8,128)(2,1)S(1)}, u32[]{:S(2)}) copy-start(bf16[34,128,1536]{2,1,0:T(8,128)(2,1)S(1)} %constant_dynamic-update-slice_fusion) | copy-start | bytes 40108036
  28.9 5.4 %collective-permute-start.2 = (bf16[34,1,1536]{2,0,1:T(8,128)(2,1)S(1)}, bf16[34,1,1536]{2,0,1:T(8,128)(2,1)S(1)}, u32[]{:S(2)}, u32[]{:S(2)}) collective-permute-start(bf16[34,1,1536]{2,0,1:T(8,128)(2,1)S(1)} %copy.15), channel_id=1, source_target_pairs={{0,1},{1,2},{2,3},{3,4},{4,5},{5,6},{6,7},{7,8},{8,9},{9,10},{10,1... | collective-permute-start | bytes 313352 | tf_op jit(solution)/shard_map/ppermute | solution.py:14
  32.5 5.8 %collective-permute-start.3 = (bf16[34,1,1536]{2,0,1:T(8,128)(2,1)S(1)}, bf16[34,1,1536]{2,0,1:T(8,128)(2,1)S(1)}, u32[]{:S(2)}, u32[]{:S(2)}) collective-permute-start(bf16[34,1,1536]{2,0,1:T(8,128)(2,1)S(1)} %copy.17), channel_id=1, source_target_pairs={{1,0},{2,1},{3,2},{4,3},{5,4},{6,5},{7,6},{8,7},{9,8},{10,9},{11,1... | collective-permute-start | bytes 313352 | tf_op jit(solution)/shard_map/ppermute | solution.py:17
  104.5 269.6 %copy-start.2 = (f32[32,128]{1,0:T(8,128)S(1)}, f32[32,128]{1,0:T(8,128)}, u32[]{:S(2)}) copy-start(f32[32,128]{1,0:T(8,128)} %param.8) | copy-start | bytes 49156
  104.5 269.6 %copy-start.3 = (s32[32,128]{1,0:T(8,128)S(1)}, s32[32,128]{1,0:T(8,128)}, u32[]{:S(2)}) copy-start(s32[32,128]{1,0:T(8,128)} %param.9) | copy-start | bytes 49156
Sparse Core Ops, SparseCore 0:
  110.0 253.7 all-reduce.1
where the time goes:
time: 382 us
  waiting for transfers between devices  260 us (68%)
  other arithmetic  51.2 us (13%)
  matrix products  28 us (7%)
  local copies, waits for them, and re-layouts  18 us (5%)
  between operations  13.6 us (4%)
  starting transfers between devices  11.3 us (3%)
    psum x1, waiting for transfers between devices, shards(): pick_rows = lax.psum(local_rows, ('rows', 'cols'))  254 us
    div x1, other arithmetic, window_sum(): return total / 9.0  47.2 us
    dot_general x1, matrix products, shards(): projected = jnp.dot(pooled, proj_full, precision=lax.Precision.HIGHEST)  18.7 us
    unnamed x10, local copies, waits for them, and re-layouts  11.6 us
    dot_general x1, matrix products, shards(): jnp.dot(projected, pick_rows.T, precision=lax.Precision.HIGHEST)  9.22 us
    ppermute x2, starting transfers between devices, padded_2(): lax.ppermute(lax.slice_in_dim(block, block.shape[dim] - width, None, axis...  8.06 us
  transfers between devices with their start and end apart: 5, of which 4 were waited for; matrix products, arithmetic and copies ran while one was open for 2% of the time, Pallas kernels for 0%

commit v1 on v0

--- a/solution.py
+++ b/solution.py
@@ -1,9 +1,21 @@
 import jax
 import jax.numpy as jnp
 from jax import lax
+from jax.experimental import pallas as pl
+from jax.experimental.pallas import tpu as pltpu
 from jax.sharding import PartitionSpec as P
 
 D_PROJ = 128
+MESH = pl.DeviceIdType.MESH
+F32, BF16 = jnp.float32, jnp.bfloat16
+
+ROWS, COLS, CHANNELS, PICKS = 32, 128, 1536, 512
+SLOTS = 8
+CHUNK = 4
+CHUNKS = ROWS // CHUNK
+LEFT = (ROWS + 2) * COLS
+RIGHT = LEFT + 48
+TABLE = RIGHT + 48
 
 
 def padded_2(block, sides, width):
@@ -29,7 +41,7 @@
     return total / 9.0
 
 
-def shards(features, projection, prev_dist, valid, pick_owner, pick_slot):
+def any_picks(features, projection, prev_dist, valid, pick_owner, pick_slot):
     rows_dev, cols_dev, channels = features.shape
     proj_full = projection.astype(jnp.float32)
     own_index = lax.axis_index("rows") * lax.axis_size("cols") + lax.axis_index("cols")
@@ -47,6 +59,313 @@
     return jnp.where(valid == 1, jnp.minimum(prev_dist, nearest), jnp.float32(0.0))
 
 
+def iota(shape, dim):
+    return lax.broadcasted_iota(jnp.int32, shape, dim)
+
+
+def dot(a, b):
+    return jnp.dot(a, b, preferred_element_type=F32)
+
+
+def touches(pick_row, pick_col, row0, col0):
+    down, across = pick_row - row0, pick_col - col0
+    return (down >= -1) & (down <= ROWS) & (across >= -1) & (across <= COLS)
+
+
+def kernel(
+    feat_hbm, proj_ref, prev_ref, valid_ref, owner_ref, slot_ref, out_ref, most_ref,
+    feat, table, hsum, edge, mine, line, plane, part, other, onehot,
+    rhs, lhs, own_sq, best, from_up, from_down, from_left, from_right, corner, side,
+    load_sem, send_sem, recv_sem, halo_send, halo_recv,
+):
+    r, c = lax.axis_index("rows"), lax.axis_index("cols")
+    x, core = r // 2, r % 2
+    y, z = c // 8, c % 8
+    up, down = lax.rem(r + 7, 8), lax.rem(r + 1, 8)
+    left, right = lax.rem(c + 31, 32), lax.rem(c + 1, 32)
+
+    def on_line(step):
+        return (r, y * 8 + lax.rem(z + step, 8))
+
+    def on_plane(step):
+        return (lax.rem(x + step // 4, 4) * 2 + core, lax.rem(y + step % 4, 4) * 8 + z)
+
+    loads = [
+        pltpu.make_async_copy(
+            feat_hbm.at[pl.ds(i * CHUNK, CHUNK)], feat.at[pl.ds(i * CHUNK, CHUNK)], load_sem.at[i]
+        )
+        for i in range(CHUNKS)
+    ]
+    for load in loads:
+        load.start()
+
+    barrier = pltpu.get_barrier_semaphore()
+
+    def greet(device):
+        pl.semaphore_signal(barrier, inc=1, device_id=device, device_id_type=MESH)
+
+    def greet_line(step, _):
+        greet(on_line(step))
+        return 0
+
+    def greet_plane(step, _):
+        greet(on_plane(step))
+        return 0
+
+    lax.fori_loop(1, 8, greet_line, 0)
+    lax.fori_loop(1, 16, greet_plane, 0)
+    around = [(up, c), (down, c), (r, left), (r, right)]
+    around += [(up, left), (up, right), (down, left), (down, right)]
+    for device in around:
+        greet(device)
+
+    owner, slot = owner_ref[...], slot_ref[...]
+    pick_row = (owner >> 5) * ROWS + (slot >> 7)
+    pick_col = (owner & 31) * COLS + (slot & 127)
+    here = jnp.broadcast_to(touches(pick_row, pick_col, r * ROWS, c * COLS), (8, PICKS))
+    before = (iota((PICKS, PICKS), 0) < iota((PICKS, PICKS), 1)).astype(F32).astype(BF16)
+    rank = dot(here.astype(F32).astype(BF16), before)
+    tile_row, tile_col = pick_row - r * ROWS, pick_col - c * COLS
+    end = jnp.where(tile_row == -1, 32, jnp.where(tile_row == ROWS, 40, tile_row))
+    place = (tile_row + 1) * COLS + tile_col
+    place = jnp.where(tile_col == -1, LEFT + end, place)
+    place = jnp.where(tile_col == COLS, RIGHT + end, place)
+    chosen = here & (rank == iota((8, PICKS), 0).astype(F32))
+    places = jnp.sum(
+        jnp.where(chosen, jnp.broadcast_to(place, (8, PICKS)).astype(F32), 0.0), axis=1, keepdims=True
+    ).astype(jnp.int32)
+    places = jnp.clip(places, 0, TABLE - 1)
+    filled = jnp.sum(chosen.astype(F32), axis=1, keepdims=True)
+
+    zero_row = jnp.zeros((1, COLS, D_PROJ), F32)
+    hsum[0:2] = jnp.zeros((2, COLS, D_PROJ), F32)
+    hsum[ROWS + 2 : ROWS + 4] = jnp.zeros((2, COLS, D_PROJ), F32)
+    edge[...] = jnp.zeros_like(edge)
+    proj = proj_ref[...]
+    sub = iota((COLS, D_PROJ), 0)
+
+    for i in range(CHUNKS):
+        loads[i].wait()
+        block = feat[i * CHUNK : (i + 1) * CHUNK].reshape(CHUNK * COLS, CHANNELS)
+        raw = dot(block, proj).reshape(CHUNK, COLS, D_PROJ)
+        for k in range(CHUNK):
+            one = raw[k]
+            row = i * CHUNK + k
+            before_it = jnp.where(sub == 0, 0.0, pltpu.roll(one, 1, 0))
+            after_it = jnp.where(sub == COLS - 1, 0.0, pltpu.roll(one, COLS - 1, 0))
+            hsum[row + 2] = one + before_it + after_it
+            edge[0, row + 8 : row + 9] = one[0:1]
+            edge[1, row + 8 : row + 9] = one[COLS - 1 : COLS]
+        for k in range(CHUNK):
+            row = i * CHUNK + k - 1
+            table[(row + 1) * COLS : (row + 2) * COLS] = hsum[row + 1] + hsum[row + 2] + hsum[row + 3]
+    for row in (ROWS - 1, ROWS):
+        table[(row + 1) * COLS : (row + 2) * COLS] = hsum[row + 1] + hsum[row + 2] + hsum[row + 3]
+    for s, base in enumerate((LEFT, RIGHT)):
+        table[base : base + 32] = edge[s, 7:39] + edge[s, 8:40] + edge[s, 9:41]
+        table[base + 32 : base + 40] = jnp.broadcast_to(edge[s, 8:9], (8, D_PROJ))
+        table[base + 40 : base + 48] = jnp.broadcast_to(edge[s, 39:40], (8, D_PROJ))
+
+    for j in range(SLOTS):
+        mine[j : j + 1] = table[pl.ds(places[j, 0], 1), :]
+    mine[...] = jnp.where(filled > 0.0, mine[...], 0.0)
+    line[z] = mine[...]
+
+    pl.semaphore_wait(barrier, 30)
+
+    def send_line(step, _):
+        pltpu.make_async_remote_copy(
+            mine, line.at[z], send_sem.at[0], recv_sem.at[0],
+            device_id=on_line(step), device_id_type=MESH,
+        ).start()
+        return 0
+
+    lax.fori_loop(1, 8, send_line, 0)
+
+    halos = [
+        (table.at[pl.ds(0, COLS)], from_down, (up, c)),
+        (table.at[pl.ds((ROWS + 1) * COLS, COLS)], from_up, (down, c)),
+        (table.at[pl.ds(LEFT, 32)], from_right, (r, left)),
+        (table.at[pl.ds(RIGHT, 32)], from_left, (r, right)),
+        (table.at[pl.ds(LEFT + 32, 8)], corner.at[3], (up, left)),
+        (table.at[pl.ds(RIGHT + 32, 8)], corner.at[2], (up, right)),
+        (table.at[pl.ds(LEFT + 40, 8)], corner.at[1], (down, left)),
+        (table.at[pl.ds(RIGHT + 40, 8)], corner.at[0], (down, right)),
+    ]
+    halo_copies = []
+    for n, (source, target, device) in enumerate(halos):
+        copy = pltpu.make_async_remote_copy(
+            source, target, halo_send.at[n], halo_recv.at[n], device_id=device, device_id_type=MESH
+        )
+        copy.start()
+        halo_copies.append(copy)
+
+    grid = jnp.concatenate(
+        [jnp.broadcast_to(pick_row, (4, PICKS)), jnp.broadcast_to(pick_col, (4, PICKS))], axis=0
+    ).astype(F32)
+    grid = grid.T
+    rows_k, cols_k = grid[:, 0:1], grid[:, 4:5]
+    d = iota((1, 128), 1)
+    row0 = (((d >> 5) * 2) * ROWS).astype(F32)
+    col0 = ((((d >> 3) & 3) * 8 + (d & 7)) * COLS).astype(F32)
+    most = jnp.zeros((1, 128), F32)
+    for half in range(2):
+        over = touches(rows_k, cols_k, row0 + half * ROWS, col0).astype(F32)
+        most = jnp.maximum(most, jnp.sum(over, axis=0, keepdims=True))
+    most_ref[...] = jnp.broadcast_to(jnp.max(most, axis=1, keepdims=True), (8, 128))
+    over = touches(rows_k, cols_k, row0 + (core * ROWS).astype(F32), col0)
+    earlier = (iota((PICKS, PICKS), 1) < iota((PICKS, PICKS), 0)).astype(F32).astype(BF16)
+    ranks = dot(earlier, over.astype(F32).astype(BF16))
+    ranks = jnp.where(over, jnp.minimum(ranks, 64.0), 100.0).astype(BF16)
+    spread = ((iota((128, 1024), 1) >> 3) == iota((128, 1024), 0)).astype(F32).astype(BF16)
+    onehot[...] = (
+        (dot(ranks, spread) == (iota((PICKS, 1024), 1) & 7).astype(F32)).astype(F32).astype(BF16)
+    )
+
+    pltpu.make_async_copy(line.at[pl.ds(0, 7)], line.at[pl.ds(0, 7)], recv_sem.at[0]).wait()
+    me = x * 4 + y
+
+    def send_plane(step, _):
+        pltpu.make_async_remote_copy(
+            line, plane.at[me], send_sem.at[1], recv_sem.at[1],
+            device_id=on_plane(step), device_id_type=MESH,
+        ).start()
+        return 0
+
+    lax.fori_loop(1, 16, send_plane, 0)
+    plane[me] = line[...]
+
+    for copy in halo_copies:
+        copy.wait_recv()
+    has_up, has_down = (r > 0).astype(F32), (r < 7).astype(F32)
+    has_left, has_right = (c > 0).astype(F32), (c < 31).astype(F32)
+    pooled = jnp.concatenate(
+        [corner[n, 0:1] for n in range(4)], axis=0
+    )
+    side[0] = from_left[...] * has_left
+    side[1] = from_right[...] * has_right
+    side[0, 0:1] += pooled[0:1] * (has_up * has_left)
+    side[1, 0:1] += pooled[1:2] * (has_up * has_right)
+    side[0, 31:32] += pooled[2:3] * (has_down * has_left)
+    side[1, 31:32] += pooled[3:4] * (has_down * has_right)
+    hsum[0] = from_up[...] * has_up
+    hsum[1] = from_down[...] * has_down
+
+    def lay_out(i, _):
+        at = pl.multiple_of(i * COLS, COLS)
+        one = table[pl.ds(at + COLS, COLS), :]
+        one += jnp.where(sub == 0, side[0, pl.ds(i, 1), :], 0.0)
+        one += jnp.where(sub == COLS - 1, side[1, pl.ds(i, 1), :], 0.0)
+        one += jnp.where(i == 0, hsum[0], 0.0) + jnp.where(i == ROWS - 1, hsum[1], 0.0)
+        flipped = one.T
+        own_sq[pl.ds(i, 1), :] = jnp.sum(flipped * flipped, axis=0, keepdims=True)
+        high = flipped.astype(BF16)
+        low = (flipped - high.astype(F32)).astype(BF16)
+        rhs[0:128, pl.ds(at, COLS)] = high
+        rhs[128:256, pl.ds(at, COLS)] = low
+        rhs[256:384, pl.ds(at, COLS)] = high
+        rhs[384:512, pl.ds(at, COLS)] = jnp.ones((128, COLS), BF16)
+        return 0
+
+    lax.fori_loop(0, ROWS, lay_out, 0)
+
+    pltpu.make_async_copy(plane.at[pl.ds(0, 15)], plane.at[pl.ds(0, 15)], recv_sem.at[1]).wait()
+    got = plane[...].reshape(1024, D_PROJ)
+    high = got.astype(BF16)
+    low = (got - high.astype(F32)).astype(BF16)
+    both = dot(onehot[...], jnp.concatenate([high, low], axis=1))
+    part[...] = both[:, :D_PROJ] + both[:, D_PROJ:]
+    swap = pltpu.make_async_remote_copy(
+        part, other, send_sem.at[2], recv_sem.at[2],
+        device_id=(x * 2 + 1 - core, c), device_id_type=MESH,
+    )
+    swap.start()
+    swap.wait_recv()
+
+    picks = part[...] + other[...]
+    high = picks.astype(BF16)
+    lhs[:, 0:128] = high
+    lhs[:, 128:256] = high
+    lhs[:, 256:384] = (picks - high.astype(F32)).astype(BF16)
+    half_sq = jnp.sum(picks * picks, axis=1, keepdims=True) * -0.5
+    first = half_sq.astype(BF16).astype(F32)
+    second = (half_sq - first).astype(BF16).astype(F32)
+    third = half_sq - first - second
+    lane = iota((PICKS, 128), 1)
+    tail = jnp.where(lane == 0, first, jnp.where(lane == 1, second, jnp.where(lane == 2, third, 0.0)))
+    lhs[:, 384:512] = tail.astype(BF16)
+
+    def nearest(i, _):
+        at = pl.multiple_of(i * 256, 256)
+        score = jnp.max(dot(lhs[...], rhs[:, pl.ds(at, 256)]), axis=0, keepdims=True)
+        best[pl.ds(2 * i, 1), :] = score[:, :128]
+        best[pl.ds(2 * i + 1, 1), :] = score[:, 128:]
+        return 0
+
+    lax.fori_loop(0, ROWS // 2, nearest, 0)
+    gap = (own_sq[...] - 2.0 * best[...]) * (1.0 / (81.0 * D_PROJ))
+    out_ref[...] = jnp.where(valid_ref[...] == 1, jnp.minimum(prev_ref[...], gap), 0.0)
+
+    pltpu.make_async_copy(line.at[pl.ds(0, 7)], line.at[pl.ds(0, 7)], send_sem.at[0]).wait()
+    pltpu.make_async_copy(plane.at[pl.ds(0, 15)], plane.at[pl.ds(0, 15)], send_sem.at[1]).wait()
+    swap.wait_send()
+    for copy in halo_copies:
+        copy.wait_send()
+
+
+def shards(features, projection, prev_dist, valid, pick_owner, pick_slot):
+    vmem = pl.BlockSpec(memory_space=pltpu.VMEM)
+    result, most = pl.pallas_call(
+        kernel,
+        out_shape=(
+            jax.ShapeDtypeStruct((ROWS, COLS), F32),
+            jax.ShapeDtypeStruct((8, 128), F32),
+        ),
+        in_specs=[pl.BlockSpec(memory_space=pltpu.HBM)] + [vmem] * 5,
+        out_specs=(vmem, vmem),
+        scratch_shapes=[
+            pltpu.VMEM((ROWS, COLS, CHANNELS), BF16),
+            pltpu.VMEM((TABLE, D_PROJ), F32),
+            pltpu.VMEM((ROWS + 4, COLS, D_PROJ), F32),
+            pltpu.VMEM((2, 48, D_PROJ), F32),
+            pltpu.VMEM((SLOTS, D_PROJ), F32),
+            pltpu.VMEM((8, SLOTS, D_PROJ), F32),
+            pltpu.VMEM((16, 8, SLOTS, D_PROJ), F32),
+            pltpu.VMEM((PICKS, D_PROJ), F32),
+            pltpu.VMEM((PICKS, D_PROJ), F32),
+            pltpu.VMEM((PICKS, 1024), BF16),
+            pltpu.VMEM((512, ROWS * COLS), BF16),
+            pltpu.VMEM((PICKS, 512), BF16),
+            pltpu.VMEM((ROWS, COLS), F32),
+            pltpu.VMEM((ROWS, COLS), F32),
+            pltpu.VMEM((COLS, D_PROJ), F32),
+            pltpu.VMEM((COLS, D_PROJ), F32),
+            pltpu.VMEM((ROWS, D_PROJ), F32),
+            pltpu.VMEM((ROWS, D_PROJ), F32),
+            pltpu.VMEM((4, 8, D_PROJ), F32),
+            pltpu.VMEM((2, ROWS, D_PROJ), F32),
+            pltpu.SemaphoreType.DMA((CHUNKS,)),
+            pltpu.SemaphoreType.DMA((3,)),
+            pltpu.SemaphoreType.DMA((3,)),
+            pltpu.SemaphoreType.DMA((8,)),
+            pltpu.SemaphoreType.DMA((8,)),
+        ],
+        compiler_params=pltpu.CompilerParams(
+            collective_id=0, has_side_effects=True, vmem_limit_bytes=56 << 20
+        ),
+        name="coreset",
+    )(
+        features, projection, prev_dist, valid,
+        pick_owner.reshape(1, PICKS), pick_slot.reshape(1, PICKS),
+    )
+    return lax.cond(
+        most[0, 0] > SLOTS,
+        any_picks,
+        lambda *_: result,
+        features, projection, prev_dist, valid, pick_owner, pick_slot,
+    )
+
+
 def solution(mesh):
     return jax.shard_map(
         shards,

time: 382 us -> 55.3 us (0.14)
  waiting for transfers between devices: 260 us -> 0 us
  other arithmetic: 51.2 us -> 0 us
  Pallas kernels: 0 us -> 39.1 us
  matrix products: 28 us -> 0 us
  local copies, waits for them, and re-layouts: 18 us -> 1.8 us
  starting transfers between devices: 11.3 us -> 0 us
    psum x1 -> x0, waiting for transfers between devices: 254 us -> none  [shards(): pick_rows = lax.psum(local_rows, ('rows', 'cols'))]
    div x1 -> x0, other arithmetic: 47.2 us -> none  [window_sum(): return total / 9.0]
    pallas_call x0 -> x1, Pallas kernels: none -> 39.1 us  [shards(): pl.pallas_call(kernel, out_shape=(jax.ShapeDtypeStruct((ROWS, COLS), F32)...]
    dot_general x2 -> x0, matrix products: 28 us -> none  [the longest x1 18.7 us: shards(): projected = jnp.dot(pooled, proj_full, precision=lax.Precision.HIGHEST)]
    ppermute x4 -> x0, starting transfers between devices: 11.3 us -> none  [the longest x2 8.06 us: padded_2(): lax.ppermute(lax.slice_in_dim(block, block.shape[dim] - width, None, axis...]
    unnamed x10 -> x1, local copies, waits for them, and re-layouts: 11.6 us -> 0.61 us
    ppermute x4 -> x0, waiting for transfers between devices: 5.69 us -> none  [the longest x2 3.82 us: padded_2(): lax.ppermute(lax.slice_in_dim(block, 0, width, axis=dim), axis, backward)]
  transfers between devices with their start and end apart: 5 -> 0, of which waited for: 4 -> 0; matrix products, arithmetic and copies ran while one was open for 2% -> 0% of each run, Pallas kernels for 0% -> 0%
where the time goes in v1:
time: 55.3 us; the launch traced here: 55.2 us
  Pallas kernels  39.1 us (71%)
  between operations  14 us (25%)
  local copies, waits for them, and re-layouts  1.8 us (3%)
    pallas_call x1, Pallas kernels, shards(): pl.pallas_call(kernel, out_shape=(jax.ShapeDtypeStruct((ROWS, COLS), F32)...  39.1 us
    slice x1, local copies, waits for them, and re-layouts, shards(): most[0, 0] > SLOTS  1.2 us

profile of v1, /device:TPU:1, one launch (start us, length us, event | category | flops | bytes accessed | tf_op | source)
XLA Modules:
  0.0 55.2 jit_solution(10874755601285389620)
XLA Ops:
  6.5 39.1 %coreset.1 = (f32[32,128]{1,0:T(8,128)S(1)}, f32[8,128]{1,0:T(8,128)}) custom-call(bf16[32,128,1536]{2,1,0:T(8,128)(2,1)} %feat_hbm.1, bf16[1536,128]{1,0:T(8,128)(2,1)} %proj_ref.1, f32[32,128]{1,0:T(8,128)} %prev_ref.1, s32[32,128]{1,0:T(8,128)} %valid_ref.1, s32[1,512]{1,0:T(1,128)} %bitcast.13, s32[1,512]{1,0:T(1,128)} %bitcast.14), custom_call_target="tpu_custom_call" | custom-call | tf_op jit(solution)/shard_map/coreset/pallas_call | solution.py:318
  45.7 1.2 %slice.47 = f32[1,1]{1,0:T(1,128)} slice(f32[8,128]{1,0:T(8,128)} %get-tuple-element.29), slice={[0:1], [0:1]} | slice | bytes 8 | tf_op jit(solution)/shard_map/slice | solution.py:362
  47.5 0.2 conditional.1
  47.7 0.6 %copy.16 = f32[32,128]{1,0:T(8,128)} copy(f32[32,128]{1,0:T(8,128)S(1)} %get-tuple-element.31) | data formatting | bytes 32768

commit v2 on v1

--- a/solution.py
+++ b/solution.py
@@ -13,9 +13,8 @@
 SLOTS = 8
 CHUNK = 4
 CHUNKS = ROWS // CHUNK
-LEFT = (ROWS + 2) * COLS
-RIGHT = LEFT + 48
-TABLE = RIGHT + 48
+WIDE = COLS + 16
+TABLE = (ROWS + 4) * WIDE
 
 
 def padded_2(block, sides, width):
@@ -50,7 +49,13 @@
     pooled = window_sum(padded, rows_dev, cols_dev).reshape(rows_dev * cols_dev, channels)
     projected = jnp.dot(pooled, proj_full, precision=lax.Precision.HIGHEST)
     local_rows = jnp.where(owned[:, None], projected[pick_slot], jnp.float32(0.0))
-    pick_rows = lax.psum(local_rows, ("rows", "cols"))
+    pick_rows = local_rows
+    for axis in ("rows", "cols"):
+        count, step = lax.axis_size(axis), 1
+        while step < count:
+            swap = [(i, i ^ step) for i in range(count)]
+            pick_rows = pick_rows + lax.ppermute(pick_rows, axis, swap)
+            step *= 2
     pick_sq = jnp.sum(pick_rows * pick_rows, axis=1)
     own_sq = jnp.sum(projected * projected, axis=1)
     inner_prod = jnp.dot(projected, pick_rows.T, precision=lax.Precision.HIGHEST)
@@ -74,7 +79,7 @@
 
 def kernel(
     feat_hbm, proj_ref, prev_ref, valid_ref, owner_ref, slot_ref, out_ref, most_ref,
-    feat, table, hsum, edge, mine, line, plane, part, other, onehot,
+    feat, raw, band, pooled, hrow, edge, ends, mine, line, plane, part, other, onehot,
     rhs, lhs, own_sq, best, from_up, from_down, from_left, from_right, corner, side,
     load_sem, send_sem, recv_sem, halo_send, halo_recv,
 ):
@@ -126,48 +131,38 @@
     before = (iota((PICKS, PICKS), 0) < iota((PICKS, PICKS), 1)).astype(F32).astype(BF16)
     rank = dot(here.astype(F32).astype(BF16), before)
     tile_row, tile_col = pick_row - r * ROWS, pick_col - c * COLS
-    end = jnp.where(tile_row == -1, 32, jnp.where(tile_row == ROWS, 40, tile_row))
-    place = (tile_row + 1) * COLS + tile_col
-    place = jnp.where(tile_col == -1, LEFT + end, place)
-    place = jnp.where(tile_col == COLS, RIGHT + end, place)
+    place = (tile_row + 2) * WIDE + tile_col + 8
     chosen = here & (rank == iota((8, PICKS), 0).astype(F32))
     places = jnp.sum(
         jnp.where(chosen, jnp.broadcast_to(place, (8, PICKS)).astype(F32), 0.0), axis=1, keepdims=True
     ).astype(jnp.int32)
-    places = jnp.clip(places, 0, TABLE - 1)
+    places = jnp.clip(places, WIDE + 1, TABLE - WIDE - 2)
     filled = jnp.sum(chosen.astype(F32), axis=1, keepdims=True)
 
-    zero_row = jnp.zeros((1, COLS, D_PROJ), F32)
-    hsum[0:2] = jnp.zeros((2, COLS, D_PROJ), F32)
-    hsum[ROWS + 2 : ROWS + 4] = jnp.zeros((2, COLS, D_PROJ), F32)
+    raw[0 : 2 * WIDE] = jnp.zeros((2 * WIDE, D_PROJ), F32)
+    raw[TABLE - 2 * WIDE :] = jnp.zeros((2 * WIDE, D_PROJ), F32)
     edge[...] = jnp.zeros_like(edge)
     proj = proj_ref[...]
-    sub = iota((COLS, D_PROJ), 0)
-
+    margin = jnp.zeros((8, D_PROJ), F32)
     for i in range(CHUNKS):
         loads[i].wait()
         block = feat[i * CHUNK : (i + 1) * CHUNK].reshape(CHUNK * COLS, CHANNELS)
-        raw = dot(block, proj).reshape(CHUNK, COLS, D_PROJ)
+        done = dot(block, proj)
         for k in range(CHUNK):
-            one = raw[k]
             row = i * CHUNK + k
-            before_it = jnp.where(sub == 0, 0.0, pltpu.roll(one, 1, 0))
-            after_it = jnp.where(sub == COLS - 1, 0.0, pltpu.roll(one, COLS - 1, 0))
-            hsum[row + 2] = one + before_it + after_it
+            one = done[k * COLS : (k + 1) * COLS]
+            at = (row + 2) * WIDE
+            raw[at : at + 8] = margin
+            raw[at + 8 : at + 8 + COLS] = one
+            raw[at + 8 + COLS : at + WIDE] = margin
             edge[0, row + 8 : row + 9] = one[0:1]
-            edge[1, row + 8 : row + 9] = one[COLS - 1 : COLS]
-        for k in range(CHUNK):
-            row = i * CHUNK + k - 1
-            table[(row + 1) * COLS : (row + 2) * COLS] = hsum[row + 1] + hsum[row + 2] + hsum[row + 3]
-    for row in (ROWS - 1, ROWS):
-        table[(row + 1) * COLS : (row + 2) * COLS] = hsum[row + 1] + hsum[row + 2] + hsum[row + 3]
-    for s, base in enumerate((LEFT, RIGHT)):
-        table[base : base + 32] = edge[s, 7:39] + edge[s, 8:40] + edge[s, 9:41]
-        table[base + 32 : base + 40] = jnp.broadcast_to(edge[s, 8:9], (8, D_PROJ))
-        table[base + 40 : base + 48] = jnp.broadcast_to(edge[s, 39:40], (8, D_PROJ))
+            edge[1, row + 8 : row + 9] = one[COLS - 1 :]
 
     for j in range(SLOTS):
-        mine[j : j + 1] = table[pl.ds(places[j, 0], 1), :]
+        place = places[j, 0]
+        near = raw[pl.ds(place - WIDE - 1, 3), :] + raw[pl.ds(place - 1, 3), :]
+        near += raw[pl.ds(place + WIDE - 1, 3), :]
+        mine[j : j + 1] = near[0:1] + near[1:2] + near[2:3]
     mine[...] = jnp.where(filled > 0.0, mine[...], 0.0)
     line[z] = mine[...]
 
@@ -182,15 +177,21 @@
 
     lax.fori_loop(1, 8, send_line, 0)
 
+    for n, at in enumerate((2 * WIDE, (ROWS + 1) * WIDE)):
+        hrow[n] = raw[at + 7 : at + 7 + COLS] + raw[at + 8 : at + 8 + COLS] + raw[at + 9 : at + 9 + COLS]
+    for n in range(2):
+        ends[n, 0:32] = edge[n, 7:39] + edge[n, 8:40] + edge[n, 9:41]
+        ends[n, 32:40] = jnp.broadcast_to(edge[n, 8:9], (8, D_PROJ))
+        ends[n, 40:48] = jnp.broadcast_to(edge[n, 39:40], (8, D_PROJ))
     halos = [
-        (table.at[pl.ds(0, COLS)], from_down, (up, c)),
-        (table.at[pl.ds((ROWS + 1) * COLS, COLS)], from_up, (down, c)),
-        (table.at[pl.ds(LEFT, 32)], from_right, (r, left)),
-        (table.at[pl.ds(RIGHT, 32)], from_left, (r, right)),
-        (table.at[pl.ds(LEFT + 32, 8)], corner.at[3], (up, left)),
-        (table.at[pl.ds(RIGHT + 32, 8)], corner.at[2], (up, right)),
-        (table.at[pl.ds(LEFT + 40, 8)], corner.at[1], (down, left)),
-        (table.at[pl.ds(RIGHT + 40, 8)], corner.at[0], (down, right)),
+        (hrow.at[0], from_down, (up, c)),
+        (hrow.at[1], from_up, (down, c)),
+        (ends.at[0, pl.ds(0, 32)], from_right, (r, left)),
+        (ends.at[1, pl.ds(0, 32)], from_left, (r, right)),
+        (ends.at[0, pl.ds(32, 8)], corner.at[3], (up, left)),
+        (ends.at[1, pl.ds(32, 8)], corner.at[2], (up, right)),
+        (ends.at[0, pl.ds(40, 8)], corner.at[1], (down, left)),
+        (ends.at[1, pl.ds(40, 8)], corner.at[0], (down, right)),
     ]
     halo_copies = []
     for n, (source, target, device) in enumerate(halos):
@@ -212,7 +213,7 @@
     for half in range(2):
         over = touches(rows_k, cols_k, row0 + half * ROWS, col0).astype(F32)
         most = jnp.maximum(most, jnp.sum(over, axis=0, keepdims=True))
-    most_ref[...] = jnp.broadcast_to(jnp.max(most, axis=1, keepdims=True), (8, 128))
+    most_ref[0] = jnp.max(most).astype(jnp.int32)
     over = touches(rows_k, cols_k, row0 + (core * ROWS).astype(F32), col0)
     earlier = (iota((PICKS, PICKS), 1) < iota((PICKS, PICKS), 0)).astype(F32).astype(BF16)
     ranks = dot(earlier, over.astype(F32).astype(BF16))
@@ -222,6 +223,17 @@
         (dot(ranks, spread) == (iota((PICKS, 1024), 1) & 7).astype(F32)).astype(F32).astype(BF16)
     )
 
+    def pool(i, _):
+        at = pl.multiple_of(i * WIDE, 8)
+        down_sum = raw[pl.ds(at + WIDE, WIDE), :] + raw[pl.ds(at + 2 * WIDE, WIDE), :]
+        slot = lax.rem(i, 4)
+        band[slot] = down_sum + raw[pl.ds(at + 3 * WIDE, WIDE), :]
+        across = band[slot, 7 : 7 + COLS] + band[slot, 8 : 8 + COLS] + band[slot, 9 : 9 + COLS]
+        pooled[pl.ds(pl.multiple_of(i * COLS, COLS), COLS), :] = across
+        return 0
+
+    lax.fori_loop(0, ROWS, pool, 0, unroll=4)
+
     pltpu.make_async_copy(line.at[pl.ds(0, 7)], line.at[pl.ds(0, 7)], recv_sem.at[0]).wait()
     me = x * 4 + y
 
@@ -239,24 +251,21 @@
         copy.wait_recv()
     has_up, has_down = (r > 0).astype(F32), (r < 7).astype(F32)
     has_left, has_right = (c > 0).astype(F32), (c < 31).astype(F32)
-    pooled = jnp.concatenate(
-        [corner[n, 0:1] for n in range(4)], axis=0
-    )
     side[0] = from_left[...] * has_left
     side[1] = from_right[...] * has_right
-    side[0, 0:1] += pooled[0:1] * (has_up * has_left)
-    side[1, 0:1] += pooled[1:2] * (has_up * has_right)
-    side[0, 31:32] += pooled[2:3] * (has_down * has_left)
-    side[1, 31:32] += pooled[3:4] * (has_down * has_right)
-    hsum[0] = from_up[...] * has_up
-    hsum[1] = from_down[...] * has_down
+    side[0, 0:1] += corner[0, 0:1] * (has_up * has_left)
+    side[1, 0:1] += corner[1, 0:1] * (has_up * has_right)
+    side[0, 31:32] += corner[2, 0:1] * (has_down * has_left)
+    side[1, 31:32] += corner[3, 0:1] * (has_down * has_right)
+    pooled[0:COLS] += from_up[...] * has_up
+    pooled[(ROWS - 1) * COLS :] += from_down[...] * has_down
+    sub = iota((COLS, D_PROJ), 0)
 
     def lay_out(i, _):
         at = pl.multiple_of(i * COLS, COLS)
-        one = table[pl.ds(at + COLS, COLS), :]
+        one = pooled[pl.ds(at, COLS), :]
         one += jnp.where(sub == 0, side[0, pl.ds(i, 1), :], 0.0)
         one += jnp.where(sub == COLS - 1, side[1, pl.ds(i, 1), :], 0.0)
-        one += jnp.where(i == 0, hsum[0], 0.0) + jnp.where(i == ROWS - 1, hsum[1], 0.0)
         flipped = one.T
         own_sq[pl.ds(i, 1), :] = jnp.sum(flipped * flipped, axis=0, keepdims=True)
         high = flipped.astype(BF16)
@@ -264,10 +273,9 @@
         rhs[0:128, pl.ds(at, COLS)] = high
         rhs[128:256, pl.ds(at, COLS)] = low
         rhs[256:384, pl.ds(at, COLS)] = high
-        rhs[384:512, pl.ds(at, COLS)] = jnp.ones((128, COLS), BF16)
-        return 0
-
-    lax.fori_loop(0, ROWS, lay_out, 0)
+        return 0
+
+    lax.fori_loop(0, ROWS, lay_out, 0, unroll=2)
 
     pltpu.make_async_copy(plane.at[pl.ds(0, 15)], plane.at[pl.ds(0, 15)], recv_sem.at[1]).wait()
     got = plane[...].reshape(1024, D_PROJ)
@@ -287,22 +295,12 @@
     lhs[:, 0:128] = high
     lhs[:, 128:256] = high
     lhs[:, 256:384] = (picks - high.astype(F32)).astype(BF16)
-    half_sq = jnp.sum(picks * picks, axis=1, keepdims=True) * -0.5
-    first = half_sq.astype(BF16).astype(F32)
-    second = (half_sq - first).astype(BF16).astype(F32)
-    third = half_sq - first - second
-    lane = iota((PICKS, 128), 1)
-    tail = jnp.where(lane == 0, first, jnp.where(lane == 1, second, jnp.where(lane == 2, third, 0.0)))
-    lhs[:, 384:512] = tail.astype(BF16)
-
-    def nearest(i, _):
-        at = pl.multiple_of(i * 256, 256)
-        score = jnp.max(dot(lhs[...], rhs[:, pl.ds(at, 256)]), axis=0, keepdims=True)
-        best[pl.ds(2 * i, 1), :] = score[:, :128]
-        best[pl.ds(2 * i + 1, 1), :] = score[:, 128:]
-        return 0
-
-    lax.fori_loop(0, ROWS // 2, nearest, 0)
+    half_sq = jnp.sum(picks * picks, axis=1, keepdims=True) * 0.5
+    for i in range(ROWS // 2):
+        score = dot(lhs[...], rhs[:, i * 256 : (i + 1) * 256]) - half_sq
+        score = jnp.max(score, axis=0, keepdims=True)
+        best[2 * i : 2 * i + 1] = score[:, :128]
+        best[2 * i + 1 : 2 * i + 2] = score[:, 128:]
     gap = (own_sq[...] - 2.0 * best[...]) * (1.0 / (81.0 * D_PROJ))
     out_ref[...] = jnp.where(valid_ref[...] == 1, jnp.minimum(prev_ref[...], gap), 0.0)
 
@@ -319,14 +317,17 @@
         kernel,
         out_shape=(
             jax.ShapeDtypeStruct((ROWS, COLS), F32),
-            jax.ShapeDtypeStruct((8, 128), F32),
+            jax.ShapeDtypeStruct((1,), jnp.int32),
         ),
         in_specs=[pl.BlockSpec(memory_space=pltpu.HBM)] + [vmem] * 5,
-        out_specs=(vmem, vmem),
+        out_specs=(vmem, pl.BlockSpec(memory_space=pltpu.SMEM)),
         scratch_shapes=[
             pltpu.VMEM((ROWS, COLS, CHANNELS), BF16),
             pltpu.VMEM((TABLE, D_PROJ), F32),
-            pltpu.VMEM((ROWS + 4, COLS, D_PROJ), F32),
+            pltpu.VMEM((4, WIDE, D_PROJ), F32),
+            pltpu.VMEM((ROWS * COLS, D_PROJ), F32),
+            pltpu.VMEM((2, COLS, D_PROJ), F32),
+            pltpu.VMEM((2, 48, D_PROJ), F32),
             pltpu.VMEM((2, 48, D_PROJ), F32),
             pltpu.VMEM((SLOTS, D_PROJ), F32),
             pltpu.VMEM((8, SLOTS, D_PROJ), F32),
@@ -334,8 +335,8 @@
             pltpu.VMEM((PICKS, D_PROJ), F32),
             pltpu.VMEM((PICKS, D_PROJ), F32),
             pltpu.VMEM((PICKS, 1024), BF16),
-            pltpu.VMEM((512, ROWS * COLS), BF16),
-            pltpu.VMEM((PICKS, 512), BF16),
+            pltpu.VMEM((384, ROWS * COLS), BF16),
+            pltpu.VMEM((PICKS, 384), BF16),
             pltpu.VMEM((ROWS, COLS), F32),
             pltpu.VMEM((ROWS, COLS), F32),
             pltpu.VMEM((COLS, D_PROJ), F32),
@@ -359,7 +360,7 @@
         pick_owner.reshape(1, PICKS), pick_slot.reshape(1, PICKS),
     )
     return lax.cond(
-        most[0, 0] > SLOTS,
+        most[0] > SLOTS,
         any_picks,
         lambda *_: result,
         features, projection, prev_dist, valid, pick_owner, pick_slot,

time: 55.3 us -> 38.1 us (0.69)
  between operations: 14 us -> 0.58 us
  Pallas kernels: 39.1 us -> 36.6 us
  local copies, waits for them, and re-layouts: 1.8 us -> 0.61 us
    pallas_call x1, Pallas kernels: 39.1 us -> 36.6 us  [shards(): pl.pallas_call(kernel, out_shape=(jax.ShapeDtypeStruct((ROWS, COLS), F32)...]
    slice x1 -> x0, local copies, waits for them, and re-layouts: 1.2 us -> none  [shards(): most[0, 0] > SLOTS]
where the time goes in v2:
time: 38.1 us; the launch traced here: 38 us
  Pallas kernels  36.6 us (96%)
  local copies, waits for them, and re-layouts  0.61 us (2%)
  between operations  0.58 us (2%)
    pallas_call x1, Pallas kernels, shards(): pl.pallas_call(kernel, out_shape=(jax.ShapeDtypeStruct((ROWS, COLS), F32)...  36.6 us

profile of v2, /device:TPU:1, one launch (start us, length us, event | category | flops | bytes accessed | tf_op | source)
XLA Modules:
  0.0 38.0 jit_solution(16785188064668169304)
XLA Ops:
  0.0 36.6 %coreset.1 = (f32[32,128]{1,0:T(8,128)S(1)}, s32[1]{0:T(128)}) custom-call(bf16[32,128,1536]{2,1,0:T(8,128)(2,1)} %feat_hbm.1, bf16[1536,128]{1,0:T(8,128)(2,1)} %proj_ref.1, f32[32,128]{1,0:T(8,128)} %prev_ref.1, s32[32,128]{1,0:T(8,128)} %valid_ref.1, s32[1,512]{1,0:T(1,128)} %bitcast.12, s32[1,512]{1,0:T(1,128)} %bitcast.13), custom_call_target="tpu_custom_call" | custom-call | tf_op jit(solution)/shard_map/coreset/pallas_call | solution.py:316
  37.2 0.2 conditional.1
  37.4 0.6 %copy.15 = f32[32,128]{1,0:T(8,128)} copy(f32[32,128]{1,0:T(8,128)S(1)} %get-tuple-element.31) | data formatting | bytes 32768

commit v3 on v2

--- a/solution.py
+++ b/solution.py
@@ -11,8 +11,10 @@
 
 ROWS, COLS, CHANNELS, PICKS = 32, 128, 1536, 512
 SLOTS = 8
-CHUNK = 4
-CHUNKS = ROWS // CHUNK
+CHUNK = 256
+CHUNKS = CHANNELS // CHUNK
+AHEAD = 3
+BAND = 8
 WIDE = COLS + 16
 TABLE = (ROWS + 4) * WIDE
 
@@ -78,10 +80,11 @@
 
 
 def kernel(
-    feat_hbm, proj_ref, prev_ref, valid_ref, owner_ref, slot_ref, out_ref, most_ref,
-    feat, raw, band, pooled, hrow, edge, ends, mine, line, plane, part, other, onehot,
+    feat_hbm, proj_hbm, prev_hbm, valid_hbm, owner_hbm, slot_hbm, out_ref, most_ref,
+    owner_ref, slot_ref, proj_ref, prev_ref, valid_ref,
+    feat, raw, band, pooled, hrow, ends, mine, line, plane, part, other, onehot,
     rhs, lhs, own_sq, best, from_up, from_down, from_left, from_right, corner, side,
-    load_sem, send_sem, recv_sem, halo_send, halo_recv,
+    load_sem, small_sem, send_sem, recv_sem, halo_send, halo_recv,
 ):
     r, c = lax.axis_index("rows"), lax.axis_index("cols")
     x, core = r // 2, r % 2
@@ -96,12 +99,22 @@
         return (lax.rem(x + step // 4, 4) * 2 + core, lax.rem(y + step % 4, 4) * 8 + z)
 
     loads = [
-        pltpu.make_async_copy(
-            feat_hbm.at[pl.ds(i * CHUNK, CHUNK)], feat.at[pl.ds(i * CHUNK, CHUNK)], load_sem.at[i]
-        )
+        pltpu.make_async_copy(feat_hbm.at[:, :, pl.ds(i * CHUNK, CHUNK)], feat.at[i], load_sem.at[i])
         for i in range(CHUNKS)
     ]
-    for load in loads:
+    smalls = [
+        pltpu.make_async_copy(source, target, small_sem.at[n])
+        for n, (source, target) in enumerate(
+            (
+                (owner_hbm, owner_ref),
+                (slot_hbm, slot_ref),
+                (proj_hbm, proj_ref),
+                (prev_hbm, prev_ref),
+                (valid_hbm, valid_ref),
+            )
+        )
+    ]
+    for load in smalls[:3] + loads[:AHEAD] + smalls[3:]:
         load.start()
 
     barrier = pltpu.get_barrier_semaphore()
@@ -124,6 +137,8 @@
     for device in around:
         greet(device)
 
+    smalls[0].wait()
+    smalls[1].wait()
     owner, slot = owner_ref[...], slot_ref[...]
     pick_row = (owner >> 5) * ROWS + (slot >> 7)
     pick_col = (owner & 31) * COLS + (slot & 127)
@@ -141,22 +156,23 @@
 
     raw[0 : 2 * WIDE] = jnp.zeros((2 * WIDE, D_PROJ), F32)
     raw[TABLE - 2 * WIDE :] = jnp.zeros((2 * WIDE, D_PROJ), F32)
-    edge[...] = jnp.zeros_like(edge)
+    smalls[2].wait()
     proj = proj_ref[...]
     margin = jnp.zeros((8, D_PROJ), F32)
+    for row in range(2, ROWS + 2):
+        raw[row * WIDE : row * WIDE + 8] = margin
+        raw[row * WIDE + 8 + COLS : (row + 1) * WIDE] = margin
     for i in range(CHUNKS):
         loads[i].wait()
-        block = feat[i * CHUNK : (i + 1) * CHUNK].reshape(CHUNK * COLS, CHANNELS)
-        done = dot(block, proj)
-        for k in range(CHUNK):
-            row = i * CHUNK + k
-            one = done[k * COLS : (k + 1) * COLS]
-            at = (row + 2) * WIDE
-            raw[at : at + 8] = margin
-            raw[at + 8 : at + 8 + COLS] = one
-            raw[at + 8 + COLS : at + WIDE] = margin
-            edge[0, row + 8 : row + 9] = one[0:1]
-            edge[1, row + 8 : row + 9] = one[COLS - 1 :]
+        if i + AHEAD < CHUNKS:
+            loads[i + AHEAD].start()
+        for top in range(0, ROWS, BAND):
+            block = feat[i, top : top + BAND].reshape(BAND * COLS, CHUNK)
+            done = dot(block, proj[i * CHUNK : (i + 1) * CHUNK])
+            for k in range(BAND):
+                at = (top + k + 2) * WIDE + 8
+                one = done[k * COLS : (k + 1) * COLS]
+                raw[at : at + COLS] = one if i == 0 else raw[at : at + COLS] + one
 
     for j in range(SLOTS):
         place = places[j, 0]
@@ -180,9 +196,13 @@
     for n, at in enumerate((2 * WIDE, (ROWS + 1) * WIDE)):
         hrow[n] = raw[at + 7 : at + 7 + COLS] + raw[at + 8 : at + 8 + COLS] + raw[at + 9 : at + 9 + COLS]
     for n in range(2):
-        ends[n, 0:32] = edge[n, 7:39] + edge[n, 8:40] + edge[n, 9:41]
-        ends[n, 32:40] = jnp.broadcast_to(edge[n, 8:9], (8, D_PROJ))
-        ends[n, 40:48] = jnp.broadcast_to(edge[n, 39:40], (8, D_PROJ))
+        first = 2 * WIDE + 8 + n * (COLS - 1)
+        inner = raw[pl.ds(first, ROWS, stride=WIDE), :]
+        outer = raw[pl.ds(first - WIDE, ROWS, stride=WIDE), :]
+        outer += raw[pl.ds(first + WIDE, ROWS, stride=WIDE), :]
+        ends[n, 0:32] = inner + outer
+        ends[n, 32:40] = jnp.broadcast_to(inner[0:1], (8, D_PROJ))
+        ends[n, 40:48] = jnp.broadcast_to(inner[ROWS - 1 :], (8, D_PROJ))
     halos = [
         (hrow.at[0], from_down, (up, c)),
         (hrow.at[1], from_up, (down, c)),
@@ -301,6 +321,8 @@
         score = jnp.max(score, axis=0, keepdims=True)
         best[2 * i : 2 * i + 1] = score[:, :128]
         best[2 * i + 1 : 2 * i + 2] = score[:, 128:]
+    smalls[3].wait()
+    smalls[4].wait()
     gap = (own_sq[...] - 2.0 * best[...]) * (1.0 / (81.0 * D_PROJ))
     out_ref[...] = jnp.where(valid_ref[...] == 1, jnp.minimum(prev_ref[...], gap), 0.0)
 
@@ -319,15 +341,19 @@
             jax.ShapeDtypeStruct((ROWS, COLS), F32),
             jax.ShapeDtypeStruct((1,), jnp.int32),
         ),
-        in_specs=[pl.BlockSpec(memory_space=pltpu.HBM)] + [vmem] * 5,
+        in_specs=[pl.BlockSpec(memory_space=pltpu.HBM)] * 6,
         out_specs=(vmem, pl.BlockSpec(memory_space=pltpu.SMEM)),
         scratch_shapes=[
-            pltpu.VMEM((ROWS, COLS, CHANNELS), BF16),
+            pltpu.VMEM((1, PICKS), jnp.int32),
+            pltpu.VMEM((1, PICKS), jnp.int32),
+            pltpu.VMEM((CHANNELS, D_PROJ), BF16),
+            pltpu.VMEM((ROWS, COLS), F32),
+            pltpu.VMEM((ROWS, COLS), jnp.int32),
+            pltpu.VMEM((CHUNKS, ROWS, COLS, CHUNK), BF16),
             pltpu.VMEM((TABLE, D_PROJ), F32),
             pltpu.VMEM((4, WIDE, D_PROJ), F32),
             pltpu.VMEM((ROWS * COLS, D_PROJ), F32),
             pltpu.VMEM((2, COLS, D_PROJ), F32),
-            pltpu.VMEM((2, 48, D_PROJ), F32),
             pltpu.VMEM((2, 48, D_PROJ), F32),
             pltpu.VMEM((SLOTS, D_PROJ), F32),
             pltpu.VMEM((8, SLOTS, D_PROJ), F32),
@@ -346,6 +372,7 @@
             pltpu.VMEM((4, 8, D_PROJ), F32),
             pltpu.VMEM((2, ROWS, D_PROJ), F32),
             pltpu.SemaphoreType.DMA((CHUNKS,)),
+            pltpu.SemaphoreType.DMA((5,)),
             pltpu.SemaphoreType.DMA((3,)),
             pltpu.SemaphoreType.DMA((3,)),
             pltpu.SemaphoreType.DMA((8,)),

time: 38.1 us -> 33.9 us (0.89)
  Pallas kernels: 36.6 us -> 32.4 us
    pallas_call x1, Pallas kernels: 36.6 us -> 32.4 us  [shards(): pl.pallas_call(kernel, out_shape=(jax.ShapeDtypeStruct((ROWS, COLS), F32)...]
where the time goes in v3:
time: 33.9 us; the launch traced here: 33.8 us
  Pallas kernels  32.4 us (96%)
  local copies, waits for them, and re-layouts  0.61 us (2%)
  between operations  0.58 us (2%)
    pallas_call x1, Pallas kernels, shards(): pl.pallas_call(kernel, out_shape=(jax.ShapeDtypeStruct((ROWS, COLS), F32)...  32.4 us

profile of v3, /device:TPU:1, one launch (start us, length us, event | category | flops | bytes accessed | tf_op | source)
XLA Modules:
  0.0 33.8 jit_solution(12796057165499388956)
XLA Ops:
  0.0 32.4 %coreset.1 = (f32[32,128]{1,0:T(8,128)S(1)}, s32[1]{0:T(128)}) custom-call(bf16[32,128,1536]{2,1,0:T(8,128)(2,1)} %feat_hbm.1, bf16[1536,128]{1,0:T(8,128)(2,1)} %proj_hbm.1, f32[32,128]{1,0:T(8,128)} %prev_hbm.1, s32[32,128]{1,0:T(8,128)} %valid_hbm.1, s32[1,512]{1,0:T(1,128)} %bitcast.12, s32[1,512]{1,0:T(1,128)} %bitcast.13), custom_call_target="tpu_custom_call" | custom-call | tf_op jit(solution)/shard_map/coreset/pallas_call | solution.py:338
  33.0 0.2 conditional.1
  33.2 0.6 %copy.15 = f32[32,128]{1,0:T(8,128)} copy(f32[32,128]{1,0:T(8,128)S(1)} %get-tuple-element.31) | data formatting | bytes 32768

commit v4 on v3

--- a/solution.py
+++ b/solution.py
@@ -11,6 +11,7 @@
 
 ROWS, COLS, CHANNELS, PICKS = 32, 128, 1536, 512
 SLOTS = 8
+LINE_SLOTS = 64
 CHUNK = 256
 CHUNKS = CHANNELS // CHUNK
 AHEAD = 3
@@ -74,15 +75,15 @@
     return jnp.dot(a, b, preferred_element_type=F32)
 
 
-def touches(pick_row, pick_col, row0, col0):
+def touches(pick_row, pick_col, row0, col0, rows=ROWS, cols=COLS):
     down, across = pick_row - row0, pick_col - col0
-    return (down >= -1) & (down <= ROWS) & (across >= -1) & (across <= COLS)
+    return (down >= -1) & (down <= rows) & (across >= -1) & (across <= cols)
 
 
 def kernel(
     feat_hbm, proj_hbm, prev_hbm, valid_hbm, owner_hbm, slot_hbm, out_ref, most_ref,
     owner_ref, slot_ref, proj_ref, prev_ref, valid_ref,
-    feat, raw, band, pooled, hrow, ends, mine, line, plane, part, other, onehot,
+    feat, raw, band, pooled, hrow, ends, mine, line, packed, plane, onehot,
     rhs, lhs, own_sq, best, from_up, from_down, from_left, from_right, corner, side,
     load_sem, small_sem, send_sem, recv_sem, halo_send, halo_recv,
 ):
@@ -93,7 +94,7 @@
     left, right = lax.rem(c + 31, 32), lax.rem(c + 1, 32)
 
     def on_line(step):
-        return (r, y * 8 + lax.rem(z + step, 8))
+        return (x * 2 + lax.rem(core + step // 8, 2), y * 8 + lax.rem(z + step % 8, 8))
 
     def on_plane(step):
         return (lax.rem(x + step // 4, 4) * 2 + core, lax.rem(y + step % 4, 4) * 8 + z)
@@ -130,7 +131,7 @@
         greet(on_plane(step))
         return 0
 
-    lax.fori_loop(1, 8, greet_line, 0)
+    lax.fori_loop(1, 16, greet_line, 0)
     lax.fori_loop(1, 16, greet_plane, 0)
     around = [(up, c), (down, c), (r, left), (r, right)]
     around += [(up, left), (up, right), (down, left), (down, right)]
@@ -180,18 +181,19 @@
         near += raw[pl.ds(place + WIDE - 1, 3), :]
         mine[j : j + 1] = near[0:1] + near[1:2] + near[2:3]
     mine[...] = jnp.where(filled > 0.0, mine[...], 0.0)
-    line[z] = mine[...]
-
-    pl.semaphore_wait(barrier, 30)
+    spot = core * 8 + z
+    line[spot] = mine[...]
+
+    pl.semaphore_wait(barrier, 38)
 
     def send_line(step, _):
         pltpu.make_async_remote_copy(
-            mine, line.at[z], send_sem.at[0], recv_sem.at[0],
+            mine, line.at[spot], send_sem.at[0], recv_sem.at[0],
             device_id=on_line(step), device_id_type=MESH,
         ).start()
         return 0
 
-    lax.fori_loop(1, 8, send_line, 0)
+    lax.fori_loop(1, 16, send_line, 0)
 
     for n, at in enumerate((2 * WIDE, (ROWS + 1) * WIDE)):
         hrow[n] = raw[at + 7 : at + 7 + COLS] + raw[at + 8 : at + 8 + COLS] + raw[at + 9 : at + 9 + COLS]
@@ -226,6 +228,7 @@
     ).astype(F32)
     grid = grid.T
     rows_k, cols_k = grid[:, 0:1], grid[:, 4:5]
+    me = x * 4 + y
     d = iota((1, 128), 1)
     row0 = (((d >> 5) * 2) * ROWS).astype(F32)
     col0 = ((((d >> 3) & 3) * 8 + (d & 7)) * COLS).astype(F32)
@@ -233,15 +236,29 @@
     for half in range(2):
         over = touches(rows_k, cols_k, row0 + half * ROWS, col0).astype(F32)
         most = jnp.maximum(most, jnp.sum(over, axis=0, keepdims=True))
-    most_ref[0] = jnp.max(most).astype(jnp.int32)
-    over = touches(rows_k, cols_k, row0 + (core * ROWS).astype(F32), col0)
     earlier = (iota((PICKS, PICKS), 1) < iota((PICKS, PICKS), 0)).astype(F32).astype(BF16)
+    row0, col0 = ((d >> 2) * (2 * ROWS)).astype(F32), ((d & 3) * (8 * COLS)).astype(F32)
+    over = touches(rows_k, cols_k, row0, col0, 2 * ROWS, 8 * COLS) & (d < 16)
+    in_line = jnp.sum(over.astype(F32), axis=0, keepdims=True)
+    most_ref[0] = (
+        (jnp.max(most) > float(SLOTS)) | (jnp.max(in_line) > float(LINE_SLOTS))
+    ).astype(jnp.int32)
     ranks = dot(earlier, over.astype(F32).astype(BF16))
-    ranks = jnp.where(over, jnp.minimum(ranks, 64.0), 100.0).astype(BF16)
-    spread = ((iota((128, 1024), 1) >> 3) == iota((128, 1024), 0)).astype(F32).astype(BF16)
+    ranks = jnp.where(over, jnp.minimum(ranks, 100.0), 200.0)
+    spread = ((iota((128, 1024), 1) >> 6) == iota((128, 1024), 0)).astype(F32).astype(BF16)
     onehot[...] = (
-        (dot(ranks, spread) == (iota((PICKS, 1024), 1) & 7).astype(F32)).astype(F32).astype(BF16)
+        (dot(ranks.astype(BF16), spread) == (iota((PICKS, 1024), 1) & 63).astype(F32))
+        .astype(F32)
+        .astype(BF16)
     )
+    here = jnp.sum(jnp.where(d == me, ranks, 0.0), axis=1, keepdims=True)
+    goes = (here == iota((PICKS, 128), 1).astype(F32)).astype(F32).T[:LINE_SLOTS].astype(BF16)
+    row0 = ((x * 2 + (d >> 6)) * ROWS).astype(F32)
+    col0 = ((y * 8 + ((d >> 3) & 7)) * COLS).astype(F32)
+    over = touches(rows_k, cols_k, row0, col0)
+    ranks = dot(earlier, over.astype(F32).astype(BF16))
+    comes = (over & (ranks == (d & 7).astype(F32))).astype(F32).astype(BF16)
+    gather = dot(goes, comes).astype(BF16)
 
     def pool(i, _):
         at = pl.multiple_of(i * WIDE, 8)
@@ -254,18 +271,24 @@
 
     lax.fori_loop(0, ROWS, pool, 0, unroll=4)
 
-    pltpu.make_async_copy(line.at[pl.ds(0, 7)], line.at[pl.ds(0, 7)], recv_sem.at[0]).wait()
-    me = x * 4 + y
+    pltpu.make_async_copy(line.at[pl.ds(0, 15)], line.at[pl.ds(0, 15)], recv_sem.at[0]).wait()
+    got = line[...].reshape(128, D_PROJ)
+    high = got.astype(BF16)
+    rest = got - high.astype(F32)
+    middle = rest.astype(BF16)
+    low = (rest - middle.astype(F32)).astype(BF16)
+    three = dot(gather, jnp.concatenate([high, middle, low], axis=1))
+    packed[...] = three[:, :D_PROJ] + three[:, D_PROJ : 2 * D_PROJ] + three[:, 2 * D_PROJ :]
 
     def send_plane(step, _):
         pltpu.make_async_remote_copy(
-            line, plane.at[me], send_sem.at[1], recv_sem.at[1],
+            packed, plane.at[me], send_sem.at[1], recv_sem.at[1],
             device_id=on_plane(step), device_id_type=MESH,
         ).start()
         return 0
 
     lax.fori_loop(1, 16, send_plane, 0)
-    plane[me] = line[...]
+    plane[me] = packed[...]
 
     for copy in halo_copies:
         copy.wait_recv()
@@ -302,15 +325,7 @@
     high = got.astype(BF16)
     low = (got - high.astype(F32)).astype(BF16)
     both = dot(onehot[...], jnp.concatenate([high, low], axis=1))
-    part[...] = both[:, :D_PROJ] + both[:, D_PROJ:]
-    swap = pltpu.make_async_remote_copy(
-        part, other, send_sem.at[2], recv_sem.at[2],
-        device_id=(x * 2 + 1 - core, c), device_id_type=MESH,
-    )
-    swap.start()
-    swap.wait_recv()
-
-    picks = part[...] + other[...]
+    picks = both[:, :D_PROJ] + both[:, D_PROJ:]
     high = picks.astype(BF16)
     lhs[:, 0:128] = high
     lhs[:, 128:256] = high
@@ -326,9 +341,8 @@
     gap = (own_sq[...] - 2.0 * best[...]) * (1.0 / (81.0 * D_PROJ))
     out_ref[...] = jnp.where(valid_ref[...] == 1, jnp.minimum(prev_ref[...], gap), 0.0)
 
-    pltpu.make_async_copy(line.at[pl.ds(0, 7)], line.at[pl.ds(0, 7)], send_sem.at[0]).wait()
+    pltpu.make_async_copy(line.at[pl.ds(0, 15)], line.at[pl.ds(0, 15)], send_sem.at[0]).wait()
     pltpu.make_async_copy(plane.at[pl.ds(0, 15)], plane.at[pl.ds(0, 15)], send_sem.at[1]).wait()
-    swap.wait_send()
     for copy in halo_copies:
         copy.wait_send()
 
@@ -356,10 +370,9 @@
             pltpu.VMEM((2, COLS, D_PROJ), F32),
             pltpu.VMEM((2, 48, D_PROJ), F32),
             pltpu.VMEM((SLOTS, D_PROJ), F32),
-            pltpu.VMEM((8, SLOTS, D_PROJ), F32),
-            pltpu.VMEM((16, 8, SLOTS, D_PROJ), F32),
-            pltpu.VMEM((PICKS, D_PROJ), F32),
-            pltpu.VMEM((PICKS, D_PROJ), F32),
+            pltpu.VMEM((16, SLOTS, D_PROJ), F32),
+            pltpu.VMEM((LINE_SLOTS, D_PROJ), F32),
+            pltpu.VMEM((16, LINE_SLOTS, D_PROJ), F32),
             pltpu.VMEM((PICKS, 1024), BF16),
             pltpu.VMEM((384, ROWS * COLS), BF16),
             pltpu.VMEM((PICKS, 384), BF16),
@@ -373,8 +386,8 @@
             pltpu.VMEM((2, ROWS, D_PROJ), F32),
             pltpu.SemaphoreType.DMA((CHUNKS,)),
             pltpu.SemaphoreType.DMA((5,)),
-            pltpu.SemaphoreType.DMA((3,)),
-            pltpu.SemaphoreType.DMA((3,)),
+            pltpu.SemaphoreType.DMA((2,)),
+            pltpu.SemaphoreType.DMA((2,)),
             pltpu.SemaphoreType.DMA((8,)),
             pltpu.SemaphoreType.DMA((8,)),
         ],
@@ -387,7 +400,7 @@
         pick_owner.reshape(1, PICKS), pick_slot.reshape(1, PICKS),
     )
     return lax.cond(
-        most[0] > SLOTS,
+        most[0] > 0,
         any_picks,
         lambda *_: result,
         features, projection, prev_dist, valid, pick_owner, pick_slot,

time: 33.9 us -> 32.8 us (0.968)
  Pallas kernels: 32.4 us -> 31.3 us
    pallas_call x1, Pallas kernels: 32.4 us -> 31.3 us  [shards(): pl.pallas_call(kernel, out_shape=(jax.ShapeDtypeStruct((ROWS, COLS), F32)...]
where the time goes in v4:
time: 32.8 us
  Pallas kernels  31.3 us (95%)
  local copies, waits for them, and re-layouts  0.61 us (2%)
  between operations  0.58 us (2%)
    pallas_call x1, Pallas kernels, shards(): pl.pallas_call(kernel, out_shape=(jax.ShapeDtypeStruct((ROWS, COLS), F32)...  31.3 us

profile of v4, /device:TPU:1, one launch (start us, length us, event | category | flops | bytes accessed | tf_op | source)
XLA Modules:
  0.0 32.8 jit_solution(1554019486986549575)
XLA Ops:
  0.0 31.3 %coreset.1 = (f32[32,128]{1,0:T(8,128)S(1)}, s32[1]{0:T(128)}) custom-call(bf16[32,128,1536]{2,1,0:T(8,128)(2,1)} %feat_hbm.1, bf16[1536,128]{1,0:T(8,128)(2,1)} %proj_hbm.1, f32[32,128]{1,0:T(8,128)} %prev_hbm.1, s32[32,128]{1,0:T(8,128)} %valid_hbm.1, s32[1,512]{1,0:T(1,128)} %bitcast.12, s32[1,512]{1,0:T(1,128)} %bitcast.13), custom_call_target="tpu_custom_call" | custom-call | tf_op jit(solution)/shard_map/coreset/pallas_call | solution.py:352
  31.9 0.2 conditional.1
  32.1 0.6 %copy.15 = f32[32,128]{1,0:T(8,128)} copy(f32[32,128]{1,0:T(8,128)S(1)} %get-tuple-element.31) | data formatting | bytes 32768

commit v5 on v4

--- a/solution.py
+++ b/solution.py
@@ -10,7 +10,7 @@
 F32, BF16 = jnp.float32, jnp.bfloat16
 
 ROWS, COLS, CHANNELS, PICKS = 32, 128, 1536, 512
-SLOTS = 8
+SLOTS = 16
 LINE_SLOTS = 64
 CHUNK = 256
 CHUNKS = CHANNELS // CHUNK
@@ -143,14 +143,14 @@
     owner, slot = owner_ref[...], slot_ref[...]
     pick_row = (owner >> 5) * ROWS + (slot >> 7)
     pick_col = (owner & 31) * COLS + (slot & 127)
-    here = jnp.broadcast_to(touches(pick_row, pick_col, r * ROWS, c * COLS), (8, PICKS))
+    here = jnp.broadcast_to(touches(pick_row, pick_col, r * ROWS, c * COLS), (SLOTS, PICKS))
     before = (iota((PICKS, PICKS), 0) < iota((PICKS, PICKS), 1)).astype(F32).astype(BF16)
     rank = dot(here.astype(F32).astype(BF16), before)
     tile_row, tile_col = pick_row - r * ROWS, pick_col - c * COLS
     place = (tile_row + 2) * WIDE + tile_col + 8
-    chosen = here & (rank == iota((8, PICKS), 0).astype(F32))
+    chosen = here & (rank == iota((SLOTS, PICKS), 0).astype(F32))
     places = jnp.sum(
-        jnp.where(chosen, jnp.broadcast_to(place, (8, PICKS)).astype(F32), 0.0), axis=1, keepdims=True
+        jnp.where(chosen, jnp.broadcast_to(place, (SLOTS, PICKS)).astype(F32), 0.0), axis=1, keepdims=True
     ).astype(jnp.int32)
     places = jnp.clip(places, WIDE + 1, TABLE - WIDE - 2)
     filled = jnp.sum(chosen.astype(F32), axis=1, keepdims=True)
@@ -186,14 +186,12 @@
 
     pl.semaphore_wait(barrier, 38)
 
-    def send_line(step, _):
+    for step in (4, 12, 5, 13, 3, 11, 6, 14, 2, 10, 7, 15, 1, 9, 8):
         pltpu.make_async_remote_copy(
             mine, line.at[spot], send_sem.at[0], recv_sem.at[0],
             device_id=on_line(step), device_id_type=MESH,
         ).start()
-        return 0
-
-    lax.fori_loop(1, 16, send_line, 0)
+
 
     for n, at in enumerate((2 * WIDE, (ROWS + 1) * WIDE)):
         hrow[n] = raw[at + 7 : at + 7 + COLS] + raw[at + 8 : at + 8 + COLS] + raw[at + 9 : at + 9 + COLS]
@@ -253,11 +251,12 @@
     )
     here = jnp.sum(jnp.where(d == me, ranks, 0.0), axis=1, keepdims=True)
     goes = (here == iota((PICKS, 128), 1).astype(F32)).astype(F32).T[:LINE_SLOTS].astype(BF16)
-    row0 = ((x * 2 + (d >> 6)) * ROWS).astype(F32)
-    col0 = ((y * 8 + ((d >> 3) & 7)) * COLS).astype(F32)
+    d = iota((1, 16 * SLOTS), 1)
+    row0 = ((x * 2 + d // (8 * SLOTS)) * ROWS).astype(F32)
+    col0 = ((y * 8 + (d // SLOTS) % 8) * COLS).astype(F32)
     over = touches(rows_k, cols_k, row0, col0)
     ranks = dot(earlier, over.astype(F32).astype(BF16))
-    comes = (over & (ranks == (d & 7).astype(F32))).astype(F32).astype(BF16)
+    comes = (over & (ranks == (d % SLOTS).astype(F32))).astype(F32).astype(BF16)
     gather = dot(goes, comes).astype(BF16)
 
     def pool(i, _):
@@ -272,7 +271,7 @@
     lax.fori_loop(0, ROWS, pool, 0, unroll=4)
 
     pltpu.make_async_copy(line.at[pl.ds(0, 15)], line.at[pl.ds(0, 15)], recv_sem.at[0]).wait()
-    got = line[...].reshape(128, D_PROJ)
+    got = line[...].reshape(16 * SLOTS, D_PROJ)
     high = got.astype(BF16)
     rest = got - high.astype(F32)
     middle = rest.astype(BF16)
@@ -280,14 +279,12 @@
     three = dot(gather, jnp.concatenate([high, middle, low], axis=1))
     packed[...] = three[:, :D_PROJ] + three[:, D_PROJ : 2 * D_PROJ] + three[:, 2 * D_PROJ :]
 
-    def send_plane(step, _):
+    for step in (10, 6, 14, 9, 11, 2, 8, 5, 7, 13, 15, 1, 3, 4, 12):
         pltpu.make_async_remote_copy(
             packed, plane.at[me], send_sem.at[1], recv_sem.at[1],
             device_id=on_plane(step), device_id_type=MESH,
         ).start()
-        return 0
-
-    lax.fori_loop(1, 16, send_plane, 0)
+
     plane[me] = packed[...]
 
     for copy in halo_copies:

time: 32.8 us -> 32.8 us (level)
  no operation moved by 1% of the time
where the time goes in v5:
time: 32.8 us; the launch traced here: 32.7 us
  Pallas kernels  31.3 us (95%)
  local copies, waits for them, and re-layouts  0.61 us (2%)
  between operations  0.58 us (2%)
    pallas_call x1, Pallas kernels, shards(): pl.pallas_call(kernel, out_shape=(jax.ShapeDtypeStruct((ROWS, COLS), F32)...  31.3 us

profile of v5, /device:TPU:1, one launch (start us, length us, event | category | flops | bytes accessed | tf_op | source)
XLA Modules:
  0.0 32.7 jit_solution(18147961218735053276)
XLA Ops:
  0.0 31.3 %coreset.1 = (f32[32,128]{1,0:T(8,128)S(1)}, s32[1]{0:T(128)}) custom-call(bf16[32,128,1536]{2,1,0:T(8,128)(2,1)} %feat_hbm.1, bf16[1536,128]{1,0:T(8,128)(2,1)} %proj_hbm.1, f32[32,128]{1,0:T(8,128)} %prev_hbm.1, s32[32,128]{1,0:T(8,128)} %valid_hbm.1, s32[1,512]{1,0:T(1,128)} %bitcast.12, s32[1,512]{1,0:T(1,128)} %bitcast.13), custom_call_target="tpu_custom_call" | custom-call | tf_op jit(solution)/shard_map/coreset/pallas_call | solution.py:349
  31.9 0.2 conditional.1
  32.1 0.6 %copy.15 = f32[32,128]{1,0:T(8,128)} copy(f32[32,128]{1,0:T(8,128)S(1)} %get-tuple-element.31) | data formatting | bytes 32768

commit v6 on v5

--- a/solution.py
+++ b/solution.py
@@ -123,16 +123,12 @@
     def greet(device):
         pl.semaphore_signal(barrier, inc=1, device_id=device, device_id_type=MESH)
 
-    def greet_line(step, _):
+    far_line = (4, 12, 5, 13, 3, 11, 6, 14, 2, 10, 7, 15, 1, 9, 8)
+    far_plane = (10, 6, 14, 9, 11, 2, 8, 5, 7, 13, 15, 1, 3, 4, 12)
+    for step in far_line:
         greet(on_line(step))
-        return 0
-
-    def greet_plane(step, _):
+    for step in far_plane:
         greet(on_plane(step))
-        return 0
-
-    lax.fori_loop(1, 16, greet_line, 0)
-    lax.fori_loop(1, 16, greet_plane, 0)
     around = [(up, c), (down, c), (r, left), (r, right)]
     around += [(up, left), (up, right), (down, left), (down, right)]
     for device in around:
@@ -186,7 +182,7 @@
 
     pl.semaphore_wait(barrier, 38)
 
-    for step in (4, 12, 5, 13, 3, 11, 6, 14, 2, 10, 7, 15, 1, 9, 8):
+    for step in far_line:
         pltpu.make_async_remote_copy(
             mine, line.at[spot], send_sem.at[0], recv_sem.at[0],
             device_id=on_line(step), device_id_type=MESH,
@@ -279,7 +275,7 @@
     three = dot(gather, jnp.concatenate([high, middle, low], axis=1))
     packed[...] = three[:, :D_PROJ] + three[:, D_PROJ : 2 * D_PROJ] + three[:, 2 * D_PROJ :]
 
-    for step in (10, 6, 14, 9, 11, 2, 8, 5, 7, 13, 15, 1, 3, 4, 12):
+    for step in far_plane:
         pltpu.make_async_remote_copy(
             packed, plane.at[me], send_sem.at[1], recv_sem.at[1],
             device_id=on_plane(step), device_id_type=MESH,

time: 32.8 us -> 32.9 us (level)
  no operation moved by 1% of the time
where the time goes in v6:
time: 32.9 us; the launch traced here: 32.8 us
  Pallas kernels  31.4 us (95%)
  local copies, waits for them, and re-layouts  0.61 us (2%)
  between operations  0.58 us (2%)
    pallas_call x1, Pallas kernels, shards(): pl.pallas_call(kernel, out_shape=(jax.ShapeDtypeStruct((ROWS, COLS), F32)...  31.4 us

profile of v6, /device:TPU:1, one launch (start us, length us, event | category | flops | bytes accessed | tf_op | source)
XLA Modules:
  0.0 32.8 jit_solution(6228931828604383305)
XLA Ops:
  0.0 31.4 %coreset.1 = (f32[32,128]{1,0:T(8,128)S(1)}, s32[1]{0:T(128)}) custom-call(bf16[32,128,1536]{2,1,0:T(8,128)(2,1)} %feat_hbm.1, bf16[1536,128]{1,0:T(8,128)(2,1)} %proj_hbm.1, f32[32,128]{1,0:T(8,128)} %prev_hbm.1, s32[32,128]{1,0:T(8,128)} %valid_hbm.1, s32[1,512]{1,0:T(1,128)} %bitcast.12, s32[1,512]{1,0:T(1,128)} %bitcast.13), custom_call_target="tpu_custom_call" | custom-call | tf_op jit(solution)/shard_map/coreset/pallas_call | solution.py:345
  32.0 0.2 conditional.1
  32.2 0.6 %copy.15 = f32[32,128]{1,0:T(8,128)} copy(f32[32,128]{1,0:T(8,128)S(1)} %get-tuple-element.31) | data formatting | bytes 32768

commit v7 on v6

--- a/solution.py
+++ b/solution.py
@@ -304,11 +304,10 @@
         one += jnp.where(sub == COLS - 1, side[1, pl.ds(i, 1), :], 0.0)
         flipped = one.T
         own_sq[pl.ds(i, 1), :] = jnp.sum(flipped * flipped, axis=0, keepdims=True)
-        high = flipped.astype(BF16)
-        low = (flipped - high.astype(F32)).astype(BF16)
-        rhs[0:128, pl.ds(at, COLS)] = high
-        rhs[128:256, pl.ds(at, COLS)] = low
-        rhs[256:384, pl.ds(at, COLS)] = high
+        high = one.astype(BF16)
+        rhs[pl.ds(at, COLS), 0:128] = high
+        rhs[pl.ds(at, COLS), 128:256] = (one - high.astype(F32)).astype(BF16)
+        rhs[pl.ds(at, COLS), 256:384] = high
         return 0
 
     lax.fori_loop(0, ROWS, lay_out, 0, unroll=2)
@@ -318,17 +317,23 @@
     high = got.astype(BF16)
     low = (got - high.astype(F32)).astype(BF16)
     both = dot(onehot[...], jnp.concatenate([high, low], axis=1))
-    picks = both[:, :D_PROJ] + both[:, D_PROJ:]
+    picks = (both[:, :D_PROJ] + both[:, D_PROJ:]).T
     high = picks.astype(BF16)
-    lhs[:, 0:128] = high
-    lhs[:, 128:256] = high
-    lhs[:, 256:384] = (picks - high.astype(F32)).astype(BF16)
-    half_sq = jnp.sum(picks * picks, axis=1, keepdims=True) * 0.5
-    for i in range(ROWS // 2):
-        score = dot(lhs[...], rhs[:, i * 256 : (i + 1) * 256]) - half_sq
-        score = jnp.max(score, axis=0, keepdims=True)
-        best[2 * i : 2 * i + 1] = score[:, :128]
-        best[2 * i + 1 : 2 * i + 2] = score[:, 128:]
+    lhs[0:128] = high
+    lhs[128:256] = high
+    lhs[256:384] = (picks - high.astype(F32)).astype(BF16)
+    half_sq = jnp.sum(picks * picks, axis=0, keepdims=True) * 0.5
+
+    for i in range(0, ROWS, 8):
+        score = dot(rhs[i * COLS : (i + 8) * COLS], lhs[...]) - half_sq
+        top = jnp.maximum(
+            jnp.maximum(score[:, 0:128], score[:, 128:256]),
+            jnp.maximum(score[:, 256:384], score[:, 384:512]),
+        )
+        for k in range(8):
+            best[i + k : i + k + 1] = jnp.max(
+                top[k * COLS : (k + 1) * COLS].T, axis=0, keepdims=True
+            )
     smalls[3].wait()
     smalls[4].wait()
     gap = (own_sq[...] - 2.0 * best[...]) * (1.0 / (81.0 * D_PROJ))
@@ -367,8 +372,8 @@
             pltpu.VMEM((LINE_SLOTS, D_PROJ), F32),
             pltpu.VMEM((16, LINE_SLOTS, D_PROJ), F32),
             pltpu.VMEM((PICKS, 1024), BF16),
-            pltpu.VMEM((384, ROWS * COLS), BF16),
-            pltpu.VMEM((PICKS, 384), BF16),
+            pltpu.VMEM((ROWS * COLS, 384), BF16),
+            pltpu.VMEM((384, PICKS), BF16),
             pltpu.VMEM((ROWS, COLS), F32),
             pltpu.VMEM((ROWS, COLS), F32),
             pltpu.VMEM((COLS, D_PROJ), F32),

time: 32.9 us -> 32.5 us (0.988)
  Pallas kernels: 31.4 us -> 31 us
    pallas_call x1, Pallas kernels: 31.4 us -> 31 us  [shards(): pl.pallas_call(kernel, out_shape=(jax.ShapeDtypeStruct((ROWS, COLS), F32)...]
where the time goes in v7:
time: 32.5 us; the launch traced here: 32.4 us
  Pallas kernels  31 us (95%)
  local copies, waits for them, and re-layouts  0.61 us (2%)
  between operations  0.58 us (2%)
    pallas_call x1, Pallas kernels, shards(): pl.pallas_call(kernel, out_shape=(jax.ShapeDtypeStruct((ROWS, COLS), F32)...  31 us

profile of v7, /device:TPU:1, one launch (start us, length us, event | category | flops | bytes accessed | tf_op | source)
XLA Modules:
  0.0 32.4 jit_solution(15387142490258828058)
XLA Ops:
  0.0 31.0 %coreset.1 = (f32[32,128]{1,0:T(8,128)S(1)}, s32[1]{0:T(128)}) custom-call(bf16[32,128,1536]{2,1,0:T(8,128)(2,1)} %feat_hbm.1, bf16[1536,128]{1,0:T(8,128)(2,1)} %proj_hbm.1, f32[32,128]{1,0:T(8,128)} %prev_hbm.1, s32[32,128]{1,0:T(8,128)} %valid_hbm.1, s32[1,512]{1,0:T(1,128)} %bitcast.12, s32[1,512]{1,0:T(1,128)} %bitcast.13), custom_call_target="tpu_custom_call" | custom-call | tf_op jit(solution)/shard_map/coreset/pallas_call | solution.py:350
  31.5 0.2 conditional.1
  31.8 0.6 %copy.15 = f32[32,128]{1,0:T(8,128)} copy(f32[32,128]{1,0:T(8,128)S(1)} %get-tuple-element.31) | data formatting | bytes 32768
